TPU v7x, 768 devices: a whole 4x8x12 slice. The times are simulated.
768 devices in a mesh: grp: 32 (over x, y), tp: 8 (over z_hi, core), pp: 3 (over z_lo).
Axes of the slice: x: 4, y: 8, z: 12 (z_hi: 4, z_lo: 3; z = z_hi * 3 + z_lo), core: 2. Of those that a mesh axis runs over, the one named last changes fastest.
Arguments:
- vision: bfloat16 [3, 2048, 3200], P('pp', 'grp'), may hold values from -6 to 6
- text_embed: bfloat16 [3, 8192, 8192], P('pp', 'grp', 'tp'), may hold values from -6 to 6
- target: int32 [3, 2048, 1], P('pp', 'grp'), may hold values from 0 to 31; in each aligned block of 64 rows (0 to 63, 64 to 127, ..., all dimensions but the last counted through in order) at most 4 rows name the same one
- slot_place: int32 [3, 32, 128], P('pp', 'grp'), may hold values from 0 to 255, as said below
- loss_mask: int32 [3, 8192], P('pp', 'grp'), may hold values from 0 to 1
- w_proj: bfloat16 [3200, 8192], P(None, 'tp'), may hold values from -0.109375 to 0.109375
- w_value: bfloat16 [8192, 1024], P('tp'), may hold values from -0.0625 to 0.0625
- cotangent: bfloat16 [3, 8192, 1024], P('pp', 'grp'), may hold values from -6 to 6
Outputs:
- values: bfloat16 [3, 8192, 1024], P('pp', ('grp', 'tp'))
- vision_grad: bfloat16 [3, 2048, 3200], P('pp', ('grp', 'tp'))
Inputs may be any that keep to these rules, and one draw needn't show every extreme that they name: `target`: within each aligned block of 64 rows of one section no rank is named more than 4 times. `slot_place`: for each section and rank, 128 distinct positions.
All inputs are finite; a program needn't handle non-finite values.
Results may differ from a plain program's by a relative error of at most 0.0049.
Values may be sent and summed in bfloat16 or wider, within the bound.
A program may use at most 32 MiB of HBM per device.

v0:
```python
import jax
import jax.numpy as jnp
from jax import lax
from jax.sharding import PartitionSpec as P


def body(vision, text_embed, target, slot_place, loss_mask, w_proj, w_value, cotangent):
    rank_count = lax.axis_size("grp")
    tensor_count = lax.axis_size("tp")
    sequence_rows = text_embed.shape[1]
    slot_total = slot_place.shape[2]
    capacity = slot_total // rank_count
    embedded = jnp.dot(vision[0], w_proj, preferred_element_type=jnp.float32).astype(jnp.bfloat16)
    slice_width = embedded.shape[1]
    target_rank = target[0, :, 0]
    onehot = (target_rank[:, None] == jnp.arange(rank_count, dtype=jnp.int32)[None, :]).astype(
        jnp.int32
    )
    earlier = jnp.cumsum(onehot, axis=0) - onehot
    rank_within = jnp.sum(earlier * onehot, axis=1)
    slot_index = target_rank * capacity + rank_within
    chooser = (jnp.arange(slot_total, dtype=jnp.int32)[:, None] == slot_index[None, :]).astype(
        jnp.bfloat16
    )
    send_rows = jnp.dot(chooser, embedded, preferred_element_type=jnp.float32).astype(jnp.bfloat16)
    send_flag = jnp.sum(chooser.astype(jnp.float32), axis=1).astype(jnp.bfloat16)
    recv_rows, recv_flag = (
        lax.all_to_all(
            send_rows.reshape(rank_count, capacity, slice_width),
            "grp",
            split_axis=0,
            concat_axis=0,
            tiled=True,
        ),
        lax.all_to_all(
            send_flag.reshape(rank_count, capacity), "grp", split_axis=0, concat_axis=0, tiled=True
        ),
    )
    recv_rows = recv_rows.reshape(slot_total, slice_width)
    recv_flag = recv_flag.reshape(slot_total)
    positions = slot_place[0, 0, :]
    placing = (jnp.arange(sequence_rows, dtype=jnp.int32)[:, None] == positions[None, :]) & (
        recv_flag[None, :] > 0.5
    )
    placing_bf = placing.astype(jnp.bfloat16)
    is_image = jnp.sum(placing.astype(jnp.float32), axis=1)
    placed = jnp.dot(placing_bf, recv_rows, preferred_element_type=jnp.float32).astype(jnp.bfloat16)
    merged = jnp.where(is_image[:, None] > 0.5, placed, text_embed[0])
    text_local = jnp.sum(loss_mask[0].astype(jnp.float32) * (1.0 - is_image))
    text_total = lax.psum(text_local, ("grp", "pp"))
    rows_out = sequence_rows // tensor_count
    partial_value = jnp.dot(merged, w_value, preferred_element_type=jnp.float32)
    summed = lax.psum(partial_value, "tp")
    value_rows = lax.dynamic_slice_in_dim(summed, lax.axis_index("tp") * rows_out, rows_out, 0)
    cot_slots = lax.dot_general(
        placing_bf, cotangent[0], (((0,), (0,)), ((), ())), preferred_element_type=jnp.float32
    ).astype(jnp.bfloat16)
    d_slots = lax.dot_general(
        cot_slots, w_value, (((1,), (1,)), ((), ())), preferred_element_type=jnp.float32
    ).astype(jnp.bfloat16)
    returned = lax.all_to_all(
        d_slots.reshape(rank_count, capacity, slice_width),
        "grp",
        split_axis=0,
        concat_axis=0,
        tiled=True,
    )
    returned = returned.reshape(slot_total, slice_width)
    d_embedded = lax.dot_general(
        chooser, returned, (((0,), (0,)), ((), ())), preferred_element_type=jnp.float32
    ).astype(jnp.bfloat16)
    grad_rows = lax.psum_scatter(
        lax.dot_general(
            d_embedded, w_proj, (((1,), (1,)), ((), ())), preferred_element_type=jnp.float32
        ),
        "tp",
        scatter_dimension=0,
        tiled=True,
    )
    loss_scale = jnp.float32(lax.axis_size("pp") * rank_count * sequence_rows) / text_total
    return (
        value_rows.astype(jnp.bfloat16)[None],
        (grad_rows * loss_scale).astype(jnp.bfloat16)[None],
    )


def solution(mesh):
    in_specs = (
        P("pp", "grp", None),
        P("pp", "grp", "tp"),
        P("pp", "grp", None),
        P("pp", "grp", None),
        P("pp", "grp"),
        P(None, "tp"),
        P("tp", None),
        P("pp", "grp", None),
    )
    out_specs = (P("pp", ("grp", "tp"), None), P("pp", ("grp", "tp"), None))
    return jax.shard_map(body, mesh=mesh, in_specs=in_specs, out_specs=out_specs, check_vma=False)
```

profile of v0, /device:TPU:1, one launch (start us, length us, event | category | flops | bytes accessed | tf_op | source)
XLA Modules:
  0.0 464.0 jit_solution(4739977207759159142)
XLA Ops:
  7.2 0.0 copy-start
  7.2 0.0 copy-start.3
  7.2 0.0 copy-start.2
  7.2 0.0 copy-start.1
  7.2 0.9 fusion.25
  8.1 0.1 reduce_window_sum.11
  8.2 0.8 select_reduce_fusion
  9.0 0.7 multiply_add_fusion
  9.7 0.1 fusion.27
  9.8 0.7 all_to_all.16
  10.5 10.5 %all-to-all-start = ((bf16[32,1,4]{2,1,0:T(2,128)(2,1)}), bf16[32,1,4]{2,1,0:T(2,128)(2,1)S(1)}, u32[]{:S(2)}, u32[]{:S(2)}) async-start(bf16[32,1,4]{2,1,0:T(2,128)(2,1)} %all_to_all.16), calls=%async_computation | async-start | bytes 32768 | tf_op jit(solution)/shard_map/all_to_all | solution.py:35
  21.0 4.4 convolution_convert_fusion.3
  25.5 0.8 reshape.45
  26.3 0.0 copy-done.3
  26.3 1.3 dynamic-slice
  27.6 2.1 all-to-all-done
  29.6 7.2 %all-to-all-start.1 = ((bf16[32,4,1024]{2,1,0:T(4,128)(2,1)}), bf16[32,4,1024]{2,1,0:T(4,128)(2,1)S(1)}, u32[]{:S(2)}, u32[]{:S(2)}) async-start(bf16[32,4,1024]{2,1,0:T(4,128)(2,1)} %reshape.45), calls=%async_computation.1 | async-start | bytes 524288 | tf_op jit(solution)/shard_map/all_to_all | solution.py:28
  36.8 0.1 compare_reduce_fusion
  36.9 0.1 gt.27
  37.0 0.0 copy-done.2
  37.0 0.1 convert_reduce_fusion
  37.1 0.6 multiply_reduce_fusion
  38.4 218.1 %psum.15 = f32[]{:T(128)} all-reduce(f32[]{:T(128)} %multiply_reduce_fusion), channel_id=1, replica_groups=mesh['grp'=32,'tp'=8,'pp'=3] {'grp','pp'}, use_global_device_ids=true, to_apply=%region_7.8 | all-reduce | flops 1 | bytes 8 | tf_op jit(solution)/shard_map/psum | solution.py:50
  256.5 0.0 copy-done
  256.5 0.0 copy-done.1
  256.5 1.0 convolution_convert_fusion.1
  257.5 0.8 reshape.47
  258.9 0.0 all-to-all-done.1
  259.0 4.6 all-to-all-start.2
  263.6 0.0 all-reduce.4.cloned.1.call-start
  263.6 0.1 reshape.46
  263.7 1.9 fusion.1
  265.6 7.6 %all-to-all-done.2 = bf16[32,4,1024]{2,1,0:T(4,128)(2,1)} async-done(((bf16[32,4,1024]{2,1,0:T(4,128)(2,1)}), bf16[32,4,1024]{2,1,0:T(4,128)(2,1)}, u32[]{:S(2)}, u32[]{:S(2)}) %all-to-all-start.2) | async-done | bytes 262176 | tf_op jit(solution)/shard_map/all_to_all | solution.py:61
  273.2 1.0 reshape.48
  274.2 6.0 %fusion.2 = f32[64,3200]{1,0:T(8,128)} fusion(bf16[3200,1024]{1,0:T(8,128)(2,1)} %param.13, bf16[128,1024]{1,0:T(8,128)(2,1)S(1)} %reshape.48, s32[64]{0:T(128)S(1)} %multiply_add_fusion), kind=kOutput, calls=%fused_computation.8 | convolution fusion | flops 436281344 | bytes 7635200 | tf_op jit(solution)/shard_map/dot_general | solution.py:73
  280.2 0.0 all-reduce.4.cloned.1.call-update
  280.2 155.4 %all-reduce.5 = bf16[256,1024]{1,0:T(8,128)(2,1)} all-reduce(f32[256,1024]{1,0:T(8,128)S(1)} %fusion.1), channel_id=1, replica_groups=mesh['grp'=32,'tp'=8,'pp'=3] {'tp'}, use_global_device_ids=true, to_apply=%region_4.5 | all-reduce | flops 262144 | bytes 1572864 | tf_op jit(solution)/shard_map/psum | solution.py:53
  435.6 1.5 fusion.15
  437.1 18.5 %all-reduce.4.cloned.1.call-done = f32[64,3200]{1,0:T(8,128)} async-done(((f32[64,3200]{1,0:T(8,128)}), f32[64,3200]{1,0:T(8,128)}) %all-reduce.4.cloned.1.call-update) | async-done | bytes 819216
  455.6 1.5 fusion.24
  (2 shorter events, 0.0 us)
Async XLA Ops:
  7.2 249.3 %copy-start = (bf16[1024,1024]{1,0:T(8,128)(2,1)S(1)}, bf16[1024,1024]{1,0:T(8,128)(2,1)}, u32[]{:S(2)}) copy-start(bf16[1024,1024]{1,0:T(8,128)(2,1)} %param.14) | copy-start | bytes 6291460
  7.2 19.1 %copy-start.3 = (s32[1,256]{1,0:T(1,128)S(1)}, s32[1,256]{1,0:T(1,128)}, u32[]{:S(2)}) copy-start(s32[1,256]{1,0:T(1,128)} %param.12) | copy-start | bytes 3076
  7.2 29.8 %copy-start.2 = (s32[1,1,128]{2,1,0:T(1,128)S(1)}, s32[1,1,128]{2,1,0:T(1,128)}, u32[]{:S(2)}) copy-start(s32[1,1,128]{2,1,0:T(1,128)} %param.11) | copy-start | bytes 1540
  7.2 249.3 %copy-start.1 = (bf16[1,256,1024]{2,1,0:T(8,128)(2,1)S(1)}, bf16[1,256,1024]{2,1,0:T(8,128)(2,1)}, u32[]{:S(2)}) copy-start(bf16[1,256,1024]{2,1,0:T(8,128)(2,1)} %param.15) | copy-start | bytes 1572868
  10.5 19.1 %all-to-all-start = ((bf16[32,1,4]{2,1,0:T(2,128)(2,1)}), bf16[32,1,4]{2,1,0:T(2,128)(2,1)S(1)}, u32[]{:S(2)}, u32[]{:S(2)}) async-start(bf16[32,1,4]{2,1,0:T(2,128)(2,1)} %all_to_all.16), calls=%async_computation | async-start | bytes 32768 | tf_op jit(solution)/shard_map/all_to_all | solution.py:35
  29.6 229.3 %all-to-all-start.1 = ((bf16[32,4,1024]{2,1,0:T(4,128)(2,1)}), bf16[32,4,1024]{2,1,0:T(4,128)(2,1)S(1)}, u32[]{:S(2)}, u32[]{:S(2)}) async-start(bf16[32,4,1024]{2,1,0:T(4,128)(2,1)} %reshape.45), calls=%async_computation.1 | async-start | bytes 524288 | tf_op jit(solution)/shard_map/all_to_all | solution.py:28
  259.0 14.2 %all-to-all-start.2 = ((bf16[32,4,1024]{2,1,0:T(4,128)(2,1)}), bf16[32,4,1024]{2,1,0:T(4,128)(2,1)}, u32[]{:S(2)}, u32[]{:S(2)}) async-start(bf16[32,4,1024]{2,1,0:T(4,128)(2,1)} %reshape.47), calls=%async_computation.2 | async-start | bytes 524288 | tf_op jit(solution)/shard_map/all_to_all | solution.py:61
  263.6 192.0 %all-reduce.4.cloned.1.call-start = ((), (), s32[]{:S(2)}) async-start(), calls=%async_computation.3 | async-start | bytes 1638400
Sparse Core Ops, SparseCore 0:
  280.3 175.2 all-reduce.3
where the time goes:
time: 465 us; the launch traced here: 464 us
  blocking collectives  374 us (80%)
  waiting for transfers between devices  28.2 us (6%)
  starting transfers between devices  22.3 us (5%)
  between operations  15.5 us (3%)
  matrix products  13.3 us (3%)
  local copies, waits for them, and re-layouts  6.28 us (1%)
  other arithmetic  4.9 us (1%)
    psum x1, blocking collectives, body(): text_total = lax.psum(text_local, ('grp', 'pp'))  218 us
    psum x1, blocking collectives, body(): summed = lax.psum(partial_value, 'tp')  155 us
    unnamed x2, waiting for transfers between devices  18.5 us
    all_to_all x1, starting transfers between devices, body(): lax.all_to_all(send_flag.reshape(rank_count, capacity), 'grp', split_axis...  10.5 us
  transfers between devices with their start and end apart: 4, of which 3 were waited for; matrix products, arithmetic and copies ran while one was open for 3% of the time, Pallas kernels for 0%

commit v1 on v0

v1 whole, which is shorter than its diff:
```python
import functools

import jax
import jax.numpy as jnp
from jax import lax
from jax.experimental import pallas as pl
from jax.experimental.pallas import tpu as pltpu
from jax.sharding import PartitionSpec as P

MESH = pl.DeviceIdType.MESH
BF, F32, I32 = jnp.bfloat16, jnp.float32, jnp.int32


def iota(shape, dim):
    return lax.broadcasted_iota(I32, shape, dim)


def mm(a, b):
    return jnp.dot(a, b, preferred_element_type=F32)


def mm_nt(a, b):
    return lax.dot_general(a, b, (((1,), (1,)), ((), ())), preferred_element_type=F32)


def flag(cond):
    return jnp.where(cond, 1.0, 0.0).astype(F32)


def to_col(row):
    n = row.shape[1]
    return jnp.sum(jnp.where(iota((n, n), 0) == iota((n, n), 1), row, 0), axis=1, keepdims=True)


class Reduce:
    def __init__(self, env, half, pf, pb, pr, sb, r1, fdn, fup, send, recv):
        self.env, self.half = env, half
        self.pf, self.pb, self.pr, self.sb = pf, pb, pr, sb
        core, hi = env["core"], env["hi"]
        h_up, h_dn, h_op = env["h_up"], env["h_dn"], env["h_op"]
        own = lambda h, s: half(sb.at[h], s)
        self.pair = pltpu.make_async_remote_copy(
            pb, pr, send.at[6], recv.at[6], device_id={"tp": env["partner"]}, device_id_type=MESH
        )
        table = [
            (own(h_op, 0), half(r1, 0), "up"),
            (own(h_op, 1), half(r1, 1), "dn"),
            (own(h_up, 1), half(fdn, 1), "up"),
            (own(h_dn, 0), half(fup, 0), "dn"),
            (own(h_up, 0), half(fdn, 0), "up"),
            (own(h_dn, 1), half(fup, 1), "dn"),
        ]
        self.copies = [
            pltpu.make_async_remote_copy(
                src, dst, send.at[i], recv.at[i], device_id={"tp": env[way]}, device_id_type=MESH
            )
            for i, (src, dst, way) in enumerate(table)
        ]
        self.r1, self.fdn, self.fup = r1, fdn, fup

    def start_pair(self):
        self.pb[...] = self.pf[1 - self.env["core"]].astype(BF)
        self.pair.start()

    def begin(self):
        env, half = self.env, self.half
        mine = self.pf.at[env["core"]]
        self.pair.wait_recv()
        for h, s, i in (("h_op", 0, 0), ("h_op", 1, 1), ("h_up", 1, 2), ("h_dn", 0, 3)):
            v = half(mine.at[env[h]], s)[...] + half(self.pr.at[env[h]], s)[...].astype(F32)
            half(self.sb.at[env[h]], s)[...] = v.astype(BF)
            self.copies[i].start()

    def middle(self):
        env, half = self.env, self.half
        mine = self.pf.at[env["core"]]
        for h, s, i in (("h_up", 0, 0), ("h_dn", 1, 1)):
            v = half(mine.at[env[h]], s)[...] + half(self.pr.at[env[h]], s)[...].astype(F32)
            self.copies[i].wait_recv()
            v = v + half(self.r1, s)[...].astype(F32)
            half(self.sb.at[env[h]], s)[...] = v.astype(BF)
            self.copies[4 + i].start()

    def end(self):
        env = self.env
        for i in (2, 3, 4, 5):
            self.copies[i].wait_recv()
        return (
            self.pf[env["core"], env["hi"]]
            + self.pr[env["hi"]].astype(F32)
            + self.fdn[...].astype(F32)
            + self.fup[...].astype(F32)
        )

    def drain(self):
        self.pair.wait_send()
        for c in self.copies:
            c.wait_send()


def kernel(
    sizes, target, place, loss, vision, w_proj, w_value, text, cot, values_out, grad_out,
    target_v, place_v, loss_v, vision_v, wp_v, wv_v, text_v, cot_v,
    emb_acc, tpf, tpb, tpr, tsb, tr1, tfd, tfu,
    ipf, ipb, ipr, isb, ir1, ifd, ifu,
    gpf, gpb, gpr, gsb, gr1, gfd, gfu,
    xcot, rcot, xmeta, rmeta, ximg, rimg, chalf, zs, zr, tot_s, tot_r,
    load_sem, t_send, t_recv, i_send, i_recv, g_send, g_recv, a_send, a_recv, z_send, z_recv, s_sem, p_send, p_recv,
):
    groups, tps, pps, parts = sizes
    grp, tp, pp = lax.axis_index("grp"), lax.axis_index("tp"), lax.axis_index("pp")
    core, hi = lax.rem(tp, 2), tp // 2
    chips = tps // 2
    env = dict(
        core=core, hi=hi, partner=tp + 1 - 2 * core,
        up=lax.rem(tp + 2, tps), dn=lax.rem(tp + tps - 2, tps),
        h_up=lax.rem(hi + 1, chips), h_dn=lax.rem(hi + chips - 1, chips), h_op=lax.rem(hi + 2, chips),
    )
    img, width = vision_v.shape[0], wp_v.shape[1]
    dvis, seq, kvd = wp_v.shape[0], text_v.shape[0], wv_v.shape[1]
    half_kv = kvd // 2
    slots = place_v.shape[1]
    cap = slots // groups
    kchunk = dvis // parts

    pairs = [
        (target, target_v), (place, place_v), (loss, loss_v), (w_value, wv_v), (text.at[0], text_v),
        (cot.at[0, :, pl.ds(pl.multiple_of(core * half_kv, 128), half_kv)], cot_v), (vision.at[0], vision_v),
    ] + [(w_proj.at[pl.ds(i * kchunk, kchunk)], wp_v.at[pl.ds(i * kchunk, kchunk)]) for i in range(parts)]
    loads = [pltpu.make_async_copy(s, d, load_sem.at[i]) for i, (s, d) in enumerate(pairs)]
    for c in loads:
        c.start()
    barrier = pltpu.get_barrier_semaphore()

    def greet(axis, me, n):
        @pl.loop(1, n)
        def _(i):
            pl.semaphore_signal(barrier, inc=1, device_id={axis: lax.rem(me + i, n)}, device_id_type=MESH)

    greet("tp", tp, tps)
    greet("grp", grp, groups)
    greet("pp", pp, pps)

    for c in loads[:3]:
        c.wait()
    t_row = target_v[...]
    t_col = to_col(t_row)
    same = t_col == t_row
    k_col = jnp.sum(jnp.where(same & (iota((img, img), 1) < iota((img, img), 0)), 1, 0), axis=1, keepdims=True)
    k_row = jnp.sum(jnp.where(same & (iota((img, img), 0) < iota((img, img), 1)), 1, 0), axis=0, keepdims=True)
    counts = jnp.sum(flag(t_col == iota((img, 128), 1)), axis=0, keepdims=True)
    sp_row = place_v[...]
    sp_col = to_col(sp_row)
    loss_f = loss_v[...].astype(F32)
    at_slot = flag(sp_col == iota((slots, seq), 1))
    mask_slot = jnp.sum(at_slot * loss_f, axis=1, keepdims=True)
    eye = iota((slots, slots), 0) == iota((slots, slots), 1)
    mask_row = jnp.sum(jnp.where(eye, mask_slot, 0.0), axis=0, keepdims=True)
    mask_sum = jnp.sum(loss_f, axis=1, keepdims=True)
    r8 = iota((8, 128), 0)
    meta = jnp.where(r8 == 0, counts, jnp.where(r8 == 1, mask_row, jnp.where(r8 == 2, mask_sum, 0.0)))
    xmeta[...] = meta

    loads[5].wait()
    y = mm(at_slot.astype(BF), cot_v[...]).astype(BF)
    ystack = jnp.concatenate([y[:, 128 * j : 128 * (j + 1)] for j in range(4)], axis=0)
    d_i, d_l = iota((4 * slots, 4 * slots), 0), iota((4 * slots, 4 * slots), 1)
    shuffle = flag(d_l == slots * ((d_i // 4) % 4) + 4 * (d_i // 16) + d_i % 4).astype(BF)
    xcot[...] = mm(shuffle, ystack).astype(BF).reshape(groups, 16, 128)

    loads[3].wait()
    loads[4].wait()
    rows_out = seq // tps
    hr = rows_out // 2
    for n in range(4):
        cols = pl.ds(n * 256, 256)
        res = mm(text_v[...], wv_v[:, cols])
        for t in range(tps):
            for s in range(2):
                r0 = t * rows_out + s * hr
                tpf[t % 2, t // 2, s, :, cols] = res[r0 : r0 + hr]

    loads[6].wait()
    for i in range(parts):
        loads[7 + i].wait()
        part = mm(vision_v[:, i * kchunk : (i + 1) * kchunk], wp_v[i * kchunk : (i + 1) * kchunk, :])
        if i == 0:
            emb_acc[...] = part
        else:
            emb_acc[...] += part
    emb = emb_acc[...].astype(BF)
    for t in range(tps):
        if t % 2 == 0:
            res = mm(emb, wv_v[:, 128 * t : 128 * t + 256])
        piece = res[:, 128 * (t % 2) : 128 * (t % 2) + 128]
        for s in range(2):
            ipf[t % 2, t // 2, s] = piece[s * (img // 2) : (s + 1) * (img // 2)]

    by_lead = lambda ref, s: ref.at[s]
    cut = gsb.shape[-1] // 256 * 128 + 128 * (gsb.shape[-1] // 128 % 2)
    by_lane = lambda ref, s: ref.at[:, pl.ds(0, cut)] if s == 0 else ref.at[:, pl.ds(cut, ref.shape[1] - cut)]
    red_i = Reduce(env, by_lead, ipf, ipb, ipr, isb, ir1, ifd, ifu, i_send, i_recv)
    red_t = Reduce(env, by_lead, tpf, tpb, tpr, tsb, tr1, tfd, tfu, t_send, t_recv)
    red_g = Reduce(env, by_lane, gpf, gpb, gpr, gsb, gr1, gfd, gfu, g_send, g_recv)

    pl.semaphore_wait(barrier, (tps - 1) + (groups - 1) + (pps - 1))

    red_i.start_pair()

    def spread(src, dst, k, whole):
        @pl.loop(1, groups)
        def _(i):
            peer = lax.rem(grp + i, groups)
            pltpu.make_async_remote_copy(
                src if whole else src.at[peer], dst.at[grp], a_send.at[k], a_recv.at[k],
                device_id={"grp": peer}, device_id_type=MESH,
            ).start()

    def collected(ref, sem, n):
        pltpu.make_async_copy(ref.at[pl.ds(0, n)], ref.at[pl.ds(0, n)], sem).wait()

    spread(xcot, rcot, 0, False)
    red_t.start_pair()
    red_i.begin()
    spread(xmeta, rmeta, 1, True)
    red_t.begin()
    red_i.middle()

    collected(rcot, a_recv.at[0], groups - 1)
    rcot[pl.ds(grp, 1)] = xcot[pl.ds(grp, 1)]
    lane = iota((img, 4 * slots), 1)
    pick = jnp.concatenate(
        [flag(lane == 16 * t_col + 4 * j + k_col).astype(BF) for j in range(4)], axis=0
    )
    got = mm(pick, rcot[...].reshape(4 * slots, 128)).astype(BF)
    mine = jnp.concatenate([got[img * j : img * (j + 1)] for j in range(4)], axis=1)
    chalf[pl.ds(core, 1)] = mine[None]
    swap = pltpu.make_async_remote_copy(
        chalf.at[core], chalf.at[core], s_sem.at[0], s_sem.at[1], device_id={"tp": env["partner"]}, device_id_type=MESH
    )
    swap.start()

    vals = red_i.end().reshape(img, 128).astype(BF)
    r_slot = flag(iota((8 * groups, img), 0) == 8 * t_row + k_row).astype(BF)
    ximg[...] = mm(r_slot, vals).reshape(groups, 8, 128).astype(BF)
    spread(ximg, rimg, 2, False)
    red_t.middle()

    swap.wait_recv()
    for n in range(0, width, 256):
        w_rows = wv_v[n : n + 256, :]
        d = mm_nt(chalf[0], w_rows[:, :half_kv]) + mm_nt(chalf[1], w_rows[:, half_kv:])
        emb_acc[:, n : n + 256] = d
    d_img = emb_acc[...].astype(BF)
    for i in range(parts):
        res = mm_nt(d_img, wp_v[i * kchunk : (i + 1) * kchunk, :])
        for t in range(tps):
            gpf[t % 2, t // 2, :, i * kchunk : (i + 1) * kchunk] = res[8 * t : 8 * t + 8]
    red_g.start_pair()

    collected(rmeta, a_recv.at[1], groups - 1)
    rmeta[pl.ds(grp, 1)] = xmeta[...][None]
    metas = rmeta[...].reshape(8 * groups, 128).astype(BF)
    e_i, e_l = iota((groups, 8 * groups), 0), iota((groups, 8 * groups), 1)
    c_mat = mm(flag(e_l == 8 * e_i).astype(BF), metas)
    m_mat = mm(flag(e_l == 8 * e_i + 1).astype(BF), metas)
    s_mat = mm(flag(e_l == 8 * e_i + 2).astype(BF), metas)
    fan = flag(iota((groups, slots), 1) // cap == iota((groups, slots), 0)).astype(BF)
    used = lax.dot_general(
        c_mat.astype(BF), fan, (((0,), (0,)), ((), ())), preferred_element_type=F32
    )[:groups]
    k_of = (iota((groups, slots), 1) % cap).astype(F32)
    lost = jnp.sum(jnp.where(k_of < used, m_mat, 0.0)).reshape(1, 1)
    total = jnp.sum(s_mat[:, 0:1]).reshape(1, 1) - lost
    tot_s[...] = jnp.broadcast_to(total, (8, 128))
    tot_copies = []
    for i in range(1, pps):
        tot_copies.append(
            pltpu.make_async_remote_copy(
                tot_s, tot_r.at[i - 1], p_send.at[i - 1], p_recv.at[i - 1],
                device_id={"pp": lax.rem(pp + i, pps)}, device_id_type=MESH,
            )
        )
        tot_copies[-1].start()
    red_g.begin()

    x_l, x_i = iota((slots, 8 * groups), 1), iota((slots, 8 * groups), 0)
    holds = (x_i == cap * (x_l // 8) + x_l % 8) & (x_l % 8 < cap)
    sp8 = jnp.sum(jnp.where(holds, sp_col + 1, 0), axis=0, keepdims=True) - 1
    c_me = jnp.sum(jnp.where(iota((groups, 128), 1) == grp, c_mat, 0.0), axis=1, keepdims=True)
    c8 = jnp.sum(jnp.where(e_l // 8 == e_i, c_me, 0.0), axis=0, keepdims=True)
    valid = (iota((1, 8 * groups), 1) % 8).astype(F32) < c8
    pos8 = jnp.where(valid, sp8, -1)
    collected(rimg, a_recv.at[2], groups - 1)
    rimg[pl.ds(grp, 1)] = ximg[pl.ds(grp, 1)]
    put = flag(iota((seq, 8 * groups), 0) == pos8).astype(BF)
    zs[...] = mm(put, rimg[...].astype(F32).reshape(8 * groups, 128).astype(BF)).astype(BF).reshape(tps, rows_out, 128)
    z_copies = []
    for i in range(1, tps):
        peer = lax.rem(tp + i, tps)
        z_copies.append(
            pltpu.make_async_remote_copy(
                zs.at[peer], zr.at[tp], z_send.at[i - 1], z_recv.at[i - 1], device_id={"tp": peer}, device_id_type=MESH
            )
        )
        z_copies[-1].start()

    red_g.middle()
    text_vals = red_t.end().reshape(rows_out, kvd)
    is_img = jnp.sum(flag(iota((rows_out, 8 * groups), 0) + rows_out * tp == pos8), axis=1, keepdims=True)
    for c in z_copies:
        c.wait_recv()
    zr[pl.ds(tp, 1)] = zs[pl.ds(tp, 1)]
    for t in range(tps):
        cols = slice(128 * t, 128 * t + 128)
        values_out[:, cols] = jnp.where(is_img > 0.5, zr[t].astype(F32), text_vals[:, cols]).astype(BF)

    for c in tot_copies:
        c.wait_recv()
    text_total = tot_s[...]
    for i in range(1, pps):
        text_total = text_total + tot_r[i - 1]
    scale = (jnp.full((8, 128), float(pps * groups * seq), F32) / text_total)[:, 0:1]
    grad_out[...] = (red_g.end() * scale).astype(BF)

    for r in (red_i, red_t, red_g):
        r.drain()
    collected(xcot, a_send.at[0], groups - 1)
    collected(rmeta, a_send.at[1], groups - 1)
    collected(ximg, a_send.at[2], groups - 1)
    swap.wait_send()
    for c in z_copies + tot_copies:
        c.wait_send()


def body(vision, text_embed, target, slot_place, loss_mask, w_proj, w_value, cotangent):
    groups, tps, pps = lax.axis_size("grp"), lax.axis_size("tp"), lax.axis_size("pp")
    img, dvis, width = vision.shape[1], vision.shape[2], w_proj.shape[1]
    seq, kvd, slots = text_embed.shape[1], w_value.shape[1], slot_place.shape[2]
    chips, parts = tps // 2, 5
    rows, grows = seq // tps, img // tps
    vm = pltpu.VMEM
    dma = lambda *s: pltpu.SemaphoreType.DMA(s)

    def reduce_bufs(chunk):
        return [
            vm((2, chips) + chunk, F32), vm((chips,) + chunk, BF), vm((chips,) + chunk, BF), vm((chips,) + chunk, BF),
            vm(chunk, BF), vm(chunk, BF), vm(chunk, BF),
        ]

    scratch = (
        [vm((1, img), I32), vm((1, slots), I32), vm((1, seq), I32), vm((img, dvis), BF), vm((dvis, width), BF),
         vm((width, kvd), BF), vm((seq, width), BF), vm((seq, kvd // 2), BF), vm((img, width), F32)]
        + reduce_bufs((2, rows // 2, kvd))
        + reduce_bufs((2, img // 2, 128))
        + reduce_bufs((grows, dvis))
        + [vm((groups, 16, 128), BF), vm((groups, 16, 128), BF), vm((8, 128), F32), vm((groups, 8, 128), F32),
           vm((groups, 8, 128), BF), vm((groups, 8, 128), BF), vm((2, img, kvd // 2), BF),
           vm((tps, rows, 128), BF), vm((tps, rows, 128), BF), vm((8, 128), F32), vm((pps - 1, 8, 128), F32)]
        + [dma(7 + parts), dma(7), dma(7), dma(7), dma(7), dma(7), dma(7), dma(3), dma(3),
           dma(tps - 1), dma(tps - 1), dma(2), dma(pps - 1), dma(pps - 1)]
    )
    values, grads = pl.pallas_call(
        functools.partial(kernel, (groups, tps, pps, parts)),
        out_shape=(
            jax.ShapeDtypeStruct((rows, kvd), BF),
            jax.ShapeDtypeStruct((grows, dvis), BF),
        ),
        in_specs=[pl.BlockSpec(memory_space=pl.ANY)] * 8,
        out_specs=(pl.BlockSpec(memory_space=pltpu.VMEM), pl.BlockSpec(memory_space=pltpu.VMEM)),
        scratch_shapes=scratch,
        compiler_params=pltpu.CompilerParams(
            collective_id=0, has_side_effects=True, vmem_limit_bytes=48 * 1024 * 1024
        ),
    )(
        target.reshape(1, img), slot_place.reshape(1, slots), loss_mask, vision, w_proj, w_value, text_embed, cotangent
    )
    return values[None], grads[None]


def solution(mesh):
    in_specs = (
        P("pp", "grp", None),
        P("pp", "grp", "tp"),
        P("pp", "grp", None),
        P("pp", "grp", None),
        P("pp", "grp"),
        P(None, "tp"),
        P("tp", None),
        P("pp", "grp", None),
    )
    out_specs = (P("pp", ("grp", "tp"), None), P("pp", ("grp", "tp"), None))
    return jax.shard_map(body, mesh=mesh, in_specs=in_specs, out_specs=out_specs, check_vma=False)
```

time: 465 us -> 55.1 us (0.12)
  blocking collectives: 374 us -> 0 us
  Pallas kernels: 0 us -> 46.1 us
  waiting for transfers between devices: 28.2 us -> 0 us
  starting transfers between devices: 22.3 us -> 0 us
  between operations: 15.5 us -> 0.66 us
  matrix products: 13.3 us -> 0 us
  other arithmetic: 4.9 us -> 0 us
    psum x2 -> x0, blocking collectives: 374 us -> none  [the longest x1 218 us: body(): text_total = lax.psum(text_local, ('grp', 'pp'))]
    pallas_call x0 -> x1, Pallas kernels: none -> 46.1 us  [body(): pl.pallas_call(functools.partial(kernel, (groups, tps, pps, parts)), out_...]
    all_to_all x3 -> x0, starting transfers between devices: 22.3 us -> none  [the longest x1 10.5 us: body(): lax.all_to_all(send_flag.reshape(rank_count, capacity), 'grp', split_axis...]
    unnamed x2 -> x0, waiting for transfers between devices: 18.5 us -> none
    dot_general x4 -> x0, matrix products: 13.3 us -> none  [the longest x1 5.99 us: body(): lax.dot_general(d_embedded, w_proj, (((1,), (1,)), ((), ())), preferred_e...]
    all_to_all x3 -> x0, waiting for transfers between devices: 9.67 us -> none  [the longest x1 7.61 us: body(): lax.all_to_all(d_slots.reshape(rank_count, capacity, slice_width), 'grp',...]
    unnamed x9 -> x16, local copies, waits for them, and re-layouts: 1.29 us -> 7.91 us
  transfers between devices with their start and end apart: 4 -> 0, of which waited for: 3 -> 0; matrix products, arithmetic and copies ran while one was open for 3% -> 0% of each run, Pallas kernels for 0% -> 0%
where the time goes in v1:
time: 55.1 us; the launch traced here: 54.6 us
  Pallas kernels  46.1 us (84%)
  local copies, waits for them, and re-layouts  7.91 us (14%)
  between operations  0.66 us (1%)
    pallas_call x1, Pallas kernels, body(): pl.pallas_call(functools.partial(kernel, (groups, tps, pps, parts)), out_...  46.1 us
    unnamed x16, local copies, waits for them, and re-layouts  7.91 us

profile of v1, /device:TPU:1, one launch (start us, length us, event | category | flops | bytes accessed | tf_op | source)
XLA Modules:
  0.0 54.6 jit_solution(4733198022787655635)
XLA Ops:
  0.6 0.0 copy-start
  0.6 1.6 %copy-done = bf16[1024,1024]{1,0:T(8,128)(2,1)S(1)} copy-done((bf16[1024,1024]{1,0:T(8,128)(2,1)S(1)}, bf16[1024,1024]{1,0:T(8,128)(2,1)}, u32[]{:S(2)}) %copy-start) | copy-done | bytes 2097176
  2.2 0.0 copy-start.1
  2.2 1.0 %copy-done.1 = bf16[1,256,1024]{2,1,0:T(8,128)(2,1)S(1)} copy-done((bf16[1,256,1024]{2,1,0:T(8,128)(2,1)S(1)}, bf16[1,256,1024]{2,1,0:T(8,128)(2,1)}, u32[]{:S(2)}) %copy-start.1) | copy-done | bytes 524312
  3.3 0.0 copy-start.2
  3.3 1.0 %copy-done.2 = bf16[1,256,1024]{2,1,0:T(8,128)(2,1)S(1)} copy-done((bf16[1,256,1024]{2,1,0:T(8,128)(2,1)S(1)}, bf16[1,256,1024]{2,1,0:T(8,128)(2,1)}, u32[]{:S(2)}) %copy-start.2) | copy-done | bytes 524312
  4.3 0.0 copy-start.3
  4.3 1.0 %copy-done.3 = bf16[1,64,3200]{2,1,0:T(8,128)(2,1)S(1)} copy-done((bf16[1,64,3200]{2,1,0:T(8,128)(2,1)S(1)}, bf16[1,64,3200]{2,1,0:T(8,128)(2,1)}, u32[]{:S(2)}) %copy-start.3) | copy-done | bytes 409624
  5.3 0.0 copy-start.4
  5.3 0.7 %copy-done.4 = s32[1,256]{1,0:T(1,128)S(1)} copy-done((s32[1,256]{1,0:T(1,128)S(1)}, s32[1,256]{1,0:T(1,128)}, u32[]{:S(2)}) %copy-start.4) | copy-done | bytes 1048
  6.0 0.0 copy-start.5
  6.0 0.7 %copy-done.5 = s32[1,64,1]{1,2,0:T(1,128)S(1)} copy-done((s32[1,64,1]{1,2,0:T(1,128)S(1)}, s32[1,64,1]{1,2,0:T(1,128)}, u32[]{:S(2)}) %copy-start.5) | copy-done | bytes 280
  6.6 0.0 copy-start.6
  6.6 0.7 %copy-done.6 = s32[1,1,128]{2,1,0:T(1,128)S(1)} copy-done((s32[1,1,128]{2,1,0:T(1,128)S(1)}, s32[1,1,128]{2,1,0:T(1,128)}, u32[]{:S(2)}) %copy-start.6) | copy-done | bytes 536
  7.3 46.1 %shard_map.95 = (bf16[32,1024]{1,0:T(8,128)(2,1)S(1)}, bf16[8,3200]{1,0:T(8,128)(2,1)S(1)}) custom-call(s32[1,64]{1,0:T(1,128)S(1)} %bitcast.6, s32[1,128]{1,0:T(1,128)S(1)} %bitcast.7, s32[1,256]{1,0:T(1,128)S(1)} %copy-done.4, bf16[1,64,3200]{2,1,0:T(8,128)(2,1)S(1)} %copy-done.3, bf16[3200,1024]{1,0:T(8,128)(2,1)} %w_proj.1, ...), custom_call_target="tpu_custom_call" | custom-call | tf_op jit(solution)/shard_map/pallas_call | solution.py:363
  53.4 0.6 %copy.12 = bf16[1,32,1024]{2,1,0:T(8,128)(2,1)} copy(bf16[1,32,1024]{2,1,0:T(8,128)(2,1)S(1)} %bitcast.4) | data formatting | bytes 131072
  54.0 0.6 %copy.13 = bf16[1,8,3200]{2,1,0:T(8,128)(2,1)} copy(bf16[1,8,3200]{2,1,0:T(8,128)(2,1)S(1)} %bitcast.5) | data formatting | bytes 102400
Async XLA Ops:
  0.6 1.6 %copy-start = (bf16[1024,1024]{1,0:T(8,128)(2,1)S(1)}, bf16[1024,1024]{1,0:T(8,128)(2,1)}, u32[]{:S(2)}) copy-start(bf16[1024,1024]{1,0:T(8,128)(2,1)} %w_value.1) | copy-start | bytes 6291460
  2.2 1.0 %copy-start.1 = (bf16[1,256,1024]{2,1,0:T(8,128)(2,1)S(1)}, bf16[1,256,1024]{2,1,0:T(8,128)(2,1)}, u32[]{:S(2)}) copy-start(bf16[1,256,1024]{2,1,0:T(8,128)(2,1)} %text.1) | copy-start | bytes 1572868
  3.3 1.0 %copy-start.2 = (bf16[1,256,1024]{2,1,0:T(8,128)(2,1)S(1)}, bf16[1,256,1024]{2,1,0:T(8,128)(2,1)}, u32[]{:S(2)}) copy-start(bf16[1,256,1024]{2,1,0:T(8,128)(2,1)} %cot.1) | copy-start | bytes 1572868
  4.3 1.0 %copy-start.3 = (bf16[1,64,3200]{2,1,0:T(8,128)(2,1)S(1)}, bf16[1,64,3200]{2,1,0:T(8,128)(2,1)}, u32[]{:S(2)}) copy-start(bf16[1,64,3200]{2,1,0:T(8,128)(2,1)} %vision.1) | copy-start | bytes 1228804
  5.3 0.7 %copy-start.4 = (s32[1,256]{1,0:T(1,128)S(1)}, s32[1,256]{1,0:T(1,128)}, u32[]{:S(2)}) copy-start(s32[1,256]{1,0:T(1,128)} %loss.1) | copy-start | bytes 3076
  6.0 0.7 %copy-start.5 = (s32[1,64,1]{1,2,0:T(1,128)S(1)}, s32[1,64,1]{1,2,0:T(1,128)}, u32[]{:S(2)}) copy-start(s32[1,64,1]{1,2,0:T(1,128)} %param.10) | copy-start | bytes 772
  6.6 0.7 %copy-start.6 = (s32[1,1,128]{2,1,0:T(1,128)S(1)}, s32[1,1,128]{2,1,0:T(1,128)}, u32[]{:S(2)}) copy-start(s32[1,1,128]{2,1,0:T(1,128)} %param.11) | copy-start | bytes 1540

commit v2 on v1

--- a/solution.py
+++ b/solution.py
@@ -36,19 +36,18 @@
     def __init__(self, env, half, pf, pb, pr, sb, r1, fdn, fup, send, recv):
         self.env, self.half = env, half
         self.pf, self.pb, self.pr, self.sb = pf, pb, pr, sb
-        core, hi = env["core"], env["hi"]
+        self.mine = pf.at[env["core"]]
         h_up, h_dn, h_op = env["h_up"], env["h_dn"], env["h_op"]
         own = lambda h, s: half(sb.at[h], s)
-        self.pair = pltpu.make_async_remote_copy(
-            pb, pr, send.at[6], recv.at[6], device_id={"tp": env["partner"]}, device_id_type=MESH
-        )
         table = [
             (own(h_op, 0), half(r1, 0), "up"),
             (own(h_op, 1), half(r1, 1), "dn"),
+            (own(h_dn, 0), half(fup, 0), "dn"),
             (own(h_up, 1), half(fdn, 1), "up"),
-            (own(h_dn, 0), half(fup, 0), "dn"),
             (own(h_up, 0), half(fdn, 0), "up"),
             (own(h_dn, 1), half(fup, 1), "dn"),
+            (half(pb, 0), half(pr, 0), "partner"),
+            (half(pb, 1), half(pr, 1), "partner"),
         ]
         self.copies = [
             pltpu.make_async_remote_copy(
@@ -58,42 +57,45 @@
         ]
         self.r1, self.fdn, self.fup = r1, fdn, fup
 
-    def start_pair(self):
-        self.pb[...] = self.pf[1 - self.env["core"]].astype(BF)
-        self.pair.start()
-
-    def begin(self):
-        env, half = self.env, self.half
-        mine = self.pf.at[env["core"]]
-        self.pair.wait_recv()
-        for h, s, i in (("h_op", 0, 0), ("h_op", 1, 1), ("h_up", 1, 2), ("h_dn", 0, 3)):
-            v = half(mine.at[env[h]], s)[...] + half(self.pr.at[env[h]], s)[...].astype(F32)
-            half(self.sb.at[env[h]], s)[...] = v.astype(BF)
-            self.copies[i].start()
-
-    def middle(self):
-        env, half = self.env, self.half
-        mine = self.pf.at[env["core"]]
-        for h, s, i in (("h_up", 0, 0), ("h_dn", 1, 1)):
-            v = half(mine.at[env[h]], s)[...] + half(self.pr.at[env[h]], s)[...].astype(F32)
-            self.copies[i].wait_recv()
-            v = v + half(self.r1, s)[...].astype(F32)
-            half(self.sb.at[env[h]], s)[...] = v.astype(BF)
-            self.copies[4 + i].start()
+    def start_pair(self, s):
+        half = self.half
+        half(self.pb, s)[...] = half(self.pf.at[1 - self.env["core"]], s)[...].astype(BF)
+        self.copies[6 + s].start()
+
+    def pair_sum(self, h, s):
+        half = self.half
+        return half(self.mine.at[h], s)[...] + half(self.pr.at[h], s)[...].astype(F32)
+
+    def first(self, s):
+        h = self.env["h_op"]
+        self.copies[6 + s].wait_recv()
+        self.half(self.sb.at[h], s)[...] = self.pair_sum(h, s).astype(BF)
+        self.copies[s].start()
+
+    def direct(self, s):
+        h = self.env["h_dn" if s == 0 else "h_up"]
+        self.half(self.sb.at[h], s)[...] = self.pair_sum(h, s).astype(BF)
+        self.copies[2 + s].start()
+
+    def relay(self, s):
+        h = self.env["h_up" if s == 0 else "h_dn"]
+        v = self.pair_sum(h, s)
+        self.copies[s].wait_recv()
+        self.half(self.sb.at[h], s)[...] = (v + self.half(self.r1, s)[...].astype(F32)).astype(BF)
+        self.copies[4 + s].start()
 
     def end(self):
         env = self.env
         for i in (2, 3, 4, 5):
             self.copies[i].wait_recv()
         return (
-            self.pf[env["core"], env["hi"]]
+            self.mine[env["hi"]]
             + self.pr[env["hi"]].astype(F32)
             + self.fdn[...].astype(F32)
             + self.fup[...].astype(F32)
         )
 
     def drain(self):
-        self.pair.wait_send()
         for c in self.copies:
             c.wait_send()
 
@@ -107,7 +109,7 @@
     xcot, rcot, xmeta, rmeta, ximg, rimg, chalf, zs, zr, tot_s, tot_r,
     load_sem, t_send, t_recv, i_send, i_recv, g_send, g_recv, a_send, a_recv, z_send, z_recv, s_sem, p_send, p_recv,
 ):
-    groups, tps, pps, parts = sizes
+    groups, tps, pps, parts, cut = sizes
     grp, tp, pp = lax.axis_index("grp"), lax.axis_index("tp"), lax.axis_index("pp")
     core, hi = lax.rem(tp, 2), tp // 2
     chips = tps // 2
@@ -123,23 +125,28 @@
     cap = slots // groups
     kchunk = dvis // parts
 
+    gx, gy = 4, groups // 4
+    offsets = [(dx, dy) for dx in range(gx) for dy in range(gy) if dx or dy]
+    offsets.sort(key=lambda o: -(min(o[0], gx - o[0]) + min(o[1], gy - o[1])))
+    px, py = grp // gy, lax.rem(grp, gy)
+    peers = [lax.rem(px + dx, gx) * gy + lax.rem(py + dy, gy) for dx, dy in offsets]
+
     pairs = [
-        (target, target_v), (place, place_v), (loss, loss_v), (w_value, wv_v), (text.at[0], text_v),
+        (place, place_v), (target, target_v), (loss, loss_v),
         (cot.at[0, :, pl.ds(pl.multiple_of(core * half_kv, 128), half_kv)], cot_v), (vision.at[0], vision_v),
     ] + [(w_proj.at[pl.ds(i * kchunk, kchunk)], wp_v.at[pl.ds(i * kchunk, kchunk)]) for i in range(parts)]
+    pairs += [(w_value, wv_v), (text.at[0], text_v)]
     loads = [pltpu.make_async_copy(s, d, load_sem.at[i]) for i, (s, d) in enumerate(pairs)]
     for c in loads:
         c.start()
+    l_cot, l_vision, l_proj, l_value, l_text = loads[3], loads[4], loads[5:-2], loads[-2], loads[-1]
     barrier = pltpu.get_barrier_semaphore()
-
-    def greet(axis, me, n):
-        @pl.loop(1, n)
-        def _(i):
-            pl.semaphore_signal(barrier, inc=1, device_id={axis: lax.rem(me + i, n)}, device_id_type=MESH)
-
-    greet("tp", tp, tps)
-    greet("grp", grp, groups)
-    greet("pp", pp, pps)
+    for p in peers:
+        pl.semaphore_signal(barrier, inc=1, device_id={"grp": p}, device_id_type=MESH)
+    for i in range(1, tps):
+        pl.semaphore_signal(barrier, inc=1, device_id={"tp": lax.rem(tp + i, tps)}, device_id_type=MESH)
+    for i in range(1, pps):
+        pl.semaphore_signal(barrier, inc=1, device_id={"pp": lax.rem(pp + i, pps)}, device_id_type=MESH)
 
     for c in loads[:3]:
         c.wait()
@@ -161,15 +168,55 @@
     meta = jnp.where(r8 == 0, counts, jnp.where(r8 == 1, mask_row, jnp.where(r8 == 2, mask_sum, 0.0)))
     xmeta[...] = meta
 
-    loads[5].wait()
+    d_i, d_l = iota((4 * slots, 4 * slots), 0), iota((4 * slots, 4 * slots), 1)
+    shuffle = flag(d_l == slots * ((d_i // 4) % 4) + 4 * (d_i // 16) + d_i % 4).astype(BF)
+    l_cot.wait()
     y = mm(at_slot.astype(BF), cot_v[...]).astype(BF)
     ystack = jnp.concatenate([y[:, 128 * j : 128 * (j + 1)] for j in range(4)], axis=0)
-    d_i, d_l = iota((4 * slots, 4 * slots), 0), iota((4 * slots, 4 * slots), 1)
-    shuffle = flag(d_l == slots * ((d_i // 4) % 4) + 4 * (d_i // 16) + d_i % 4).astype(BF)
     xcot[...] = mm(shuffle, ystack).astype(BF).reshape(groups, 16, 128)
 
-    loads[3].wait()
-    loads[4].wait()
+    l_vision.wait()
+    for i in range(parts):
+        l_proj[i].wait()
+        part = mm(vision_v[:, i * kchunk : (i + 1) * kchunk], wp_v[i * kchunk : (i + 1) * kchunk, :])
+        if i == 0:
+            emb_acc[...] = part
+        else:
+            emb_acc[...] += part
+    l_value.wait()
+    emb = emb_acc[...].astype(BF)
+    for t in range(tps):
+        if t % 2 == 0:
+            res = mm(emb, wv_v[:, 128 * t : 128 * t + 256])
+        piece = res[:, 128 * (t % 2) : 128 * (t % 2) + 128]
+        for s in range(2):
+            ipf[t % 2, t // 2, s] = piece[s * (img // 2) : (s + 1) * (img // 2)]
+
+    lead = lambda ref, s: ref.at[..., s, :, :] if len(ref.shape) == 4 else ref.at[s]
+    span = (pl.ds(0, cut), pl.ds(cut, dvis - cut))
+    lane_cut = lambda ref, s: ref.at[..., span[s]]
+    red_i = Reduce(env, lead, ipf, ipb, ipr, isb, ir1, ifd, ifu, i_send, i_recv)
+    red_t = Reduce(env, lead, tpf, tpb, tpr, tsb, tr1, tfd, tfu, t_send, t_recv)
+    red_g = Reduce(env, lane_cut, gpf, gpb, gpr, gsb, gr1, gfd, gfu, g_send, g_recv)
+
+    pl.semaphore_wait(barrier, (tps - 1) + (groups - 1) + (pps - 1))
+
+    red_i.start_pair(0)
+    red_i.start_pair(1)
+
+    def spread(src, dst, k, whole):
+        for p in peers:
+            pltpu.make_async_remote_copy(
+                src if whole else src.at[p], dst.at[grp], a_send.at[k], a_recv.at[k],
+                device_id={"grp": p}, device_id_type=MESH,
+            ).start()
+
+    def collected(ref, sem, n):
+        pltpu.make_async_copy(ref.at[pl.ds(0, n)], ref.at[pl.ds(0, n)], sem).wait()
+
+    spread(xcot, rcot, 0, False)
+
+    l_text.wait()
     rows_out = seq // tps
     hr = rows_out // 2
     for n in range(4):
@@ -180,58 +227,26 @@
                 r0 = t * rows_out + s * hr
                 tpf[t % 2, t // 2, s, :, cols] = res[r0 : r0 + hr]
 
-    loads[6].wait()
-    for i in range(parts):
-        loads[7 + i].wait()
-        part = mm(vision_v[:, i * kchunk : (i + 1) * kchunk], wp_v[i * kchunk : (i + 1) * kchunk, :])
-        if i == 0:
-            emb_acc[...] = part
-        else:
-            emb_acc[...] += part
-    emb = emb_acc[...].astype(BF)
-    for t in range(tps):
-        if t % 2 == 0:
-            res = mm(emb, wv_v[:, 128 * t : 128 * t + 256])
-        piece = res[:, 128 * (t % 2) : 128 * (t % 2) + 128]
-        for s in range(2):
-            ipf[t % 2, t // 2, s] = piece[s * (img // 2) : (s + 1) * (img // 2)]
-
-    by_lead = lambda ref, s: ref.at[s]
-    cut = gsb.shape[-1] // 256 * 128 + 128 * (gsb.shape[-1] // 128 % 2)
-    by_lane = lambda ref, s: ref.at[:, pl.ds(0, cut)] if s == 0 else ref.at[:, pl.ds(cut, ref.shape[1] - cut)]
-    red_i = Reduce(env, by_lead, ipf, ipb, ipr, isb, ir1, ifd, ifu, i_send, i_recv)
-    red_t = Reduce(env, by_lead, tpf, tpb, tpr, tsb, tr1, tfd, tfu, t_send, t_recv)
-    red_g = Reduce(env, by_lane, gpf, gpb, gpr, gsb, gr1, gfd, gfu, g_send, g_recv)
-
-    pl.semaphore_wait(barrier, (tps - 1) + (groups - 1) + (pps - 1))
-
-    red_i.start_pair()
-
-    def spread(src, dst, k, whole):
-        @pl.loop(1, groups)
-        def _(i):
-            peer = lax.rem(grp + i, groups)
-            pltpu.make_async_remote_copy(
-                src if whole else src.at[peer], dst.at[grp], a_send.at[k], a_recv.at[k],
-                device_id={"grp": peer}, device_id_type=MESH,
-            ).start()
-
-    def collected(ref, sem, n):
-        pltpu.make_async_copy(ref.at[pl.ds(0, n)], ref.at[pl.ds(0, n)], sem).wait()
-
-    spread(xcot, rcot, 0, False)
-    red_t.start_pair()
-    red_i.begin()
+    red_i.first(0)
+    red_i.first(1)
+    red_i.direct(0)
+    red_i.direct(1)
+    red_t.start_pair(0)
+    red_t.start_pair(1)
     spread(xmeta, rmeta, 1, True)
-    red_t.begin()
-    red_i.middle()
-
-    collected(rcot, a_recv.at[0], groups - 1)
-    rcot[pl.ds(grp, 1)] = xcot[pl.ds(grp, 1)]
+    red_t.first(0)
+    red_t.first(1)
+    red_i.relay(0)
+    red_i.relay(1)
+    red_t.direct(0)
+    red_t.direct(1)
+
     lane = iota((img, 4 * slots), 1)
     pick = jnp.concatenate(
         [flag(lane == 16 * t_col + 4 * j + k_col).astype(BF) for j in range(4)], axis=0
     )
+    collected(rcot, a_recv.at[0], groups - 1)
+    rcot[pl.ds(grp, 1)] = xcot[pl.ds(grp, 1)]
     got = mm(pick, rcot[...].reshape(4 * slots, 128)).astype(BF)
     mine = jnp.concatenate([got[img * j : img * (j + 1)] for j in range(4)], axis=1)
     chalf[pl.ds(core, 1)] = mine[None]
@@ -240,23 +255,29 @@
     )
     swap.start()
 
+    half_cols = lambda c: pl.ds(pl.multiple_of(c * half_kv, 128), half_kv)
+    for n in range(0, width, 256):
+        emb_acc[:, n : n + 256] = mm_nt(mine, wv_v[n : n + 256, half_cols(core)])
+    red_t.relay(0)
+    red_t.relay(1)
+    swap.wait_recv()
+    other = chalf[1 - core]
+    for n in range(0, width, 256):
+        emb_acc[:, n : n + 256] += mm_nt(other, wv_v[n : n + 256, half_cols(1 - core)])
+    d_img = emb_acc[...].astype(BF)
+
     vals = red_i.end().reshape(img, 128).astype(BF)
     r_slot = flag(iota((8 * groups, img), 0) == 8 * t_row + k_row).astype(BF)
     ximg[...] = mm(r_slot, vals).reshape(groups, 8, 128).astype(BF)
     spread(ximg, rimg, 2, False)
-    red_t.middle()
-
-    swap.wait_recv()
-    for n in range(0, width, 256):
-        w_rows = wv_v[n : n + 256, :]
-        d = mm_nt(chalf[0], w_rows[:, :half_kv]) + mm_nt(chalf[1], w_rows[:, half_kv:])
-        emb_acc[:, n : n + 256] = d
-    d_img = emb_acc[...].astype(BF)
-    for i in range(parts):
-        res = mm_nt(d_img, wp_v[i * kchunk : (i + 1) * kchunk, :])
-        for t in range(tps):
-            gpf[t % 2, t // 2, :, i * kchunk : (i + 1) * kchunk] = res[8 * t : 8 * t + 8]
-    red_g.start_pair()
+
+    for s, bounds in enumerate(((0, cut // 2, cut), (cut, cut + (dvis - cut) // 256 * 128, dvis))):
+        for lo, up in zip(bounds[:-1], bounds[1:]):
+            res = mm_nt(d_img, wp_v[lo:up, :])
+            for t in range(tps):
+                gpf[t % 2, t // 2, :, lo:up] = res[8 * t : 8 * t + 8]
+        red_g.start_pair(s)
+    red_g.first(0)
 
     collected(rmeta, a_recv.at[1], groups - 1)
     rmeta[pl.ds(grp, 1)] = xmeta[...][None]
@@ -281,8 +302,11 @@
                 device_id={"pp": lax.rem(pp + i, pps)}, device_id_type=MESH,
             )
         )
-        tot_copies[-1].start()
-    red_g.begin()
+    red_g.first(1)
+    for c in tot_copies:
+        c.start()
+    red_g.direct(0)
+    red_g.direct(1)
 
     x_l, x_i = iota((slots, 8 * groups), 1), iota((slots, 8 * groups), 0)
     holds = (x_i == cap * (x_l // 8) + x_l % 8) & (x_l % 8 < cap)
@@ -291,12 +315,12 @@
     c8 = jnp.sum(jnp.where(e_l // 8 == e_i, c_me, 0.0), axis=0, keepdims=True)
     valid = (iota((1, 8 * groups), 1) % 8).astype(F32) < c8
     pos8 = jnp.where(valid, sp8, -1)
+    put = flag(iota((seq, 8 * groups), 0) == pos8).astype(BF)
     collected(rimg, a_recv.at[2], groups - 1)
     rimg[pl.ds(grp, 1)] = ximg[pl.ds(grp, 1)]
-    put = flag(iota((seq, 8 * groups), 0) == pos8).astype(BF)
     zs[...] = mm(put, rimg[...].astype(F32).reshape(8 * groups, 128).astype(BF)).astype(BF).reshape(tps, rows_out, 128)
     z_copies = []
-    for i in range(1, tps):
+    for i in (4, 3, 5, 2, 6, 1, 7):
         peer = lax.rem(tp + i, tps)
         z_copies.append(
             pltpu.make_async_remote_copy(
@@ -305,7 +329,8 @@
         )
         z_copies[-1].start()
 
-    red_g.middle()
+    red_g.relay(0)
+    red_g.relay(1)
     text_vals = red_t.end().reshape(rows_out, kvd)
     is_img = jnp.sum(flag(iota((rows_out, 8 * groups), 0) + rows_out * tp == pos8), axis=1, keepdims=True)
     for c in z_copies:
@@ -338,6 +363,7 @@
     img, dvis, width = vision.shape[1], vision.shape[2], w_proj.shape[1]
     seq, kvd, slots = text_embed.shape[1], w_value.shape[1], slot_place.shape[2]
     chips, parts = tps // 2, 5
+    cut = dvis // 256 * 128
     rows, grows = seq // tps, img // tps
     vm = pltpu.VMEM
     dma = lambda *s: pltpu.SemaphoreType.DMA(s)
@@ -357,11 +383,12 @@
         + [vm((groups, 16, 128), BF), vm((groups, 16, 128), BF), vm((8, 128), F32), vm((groups, 8, 128), F32),
            vm((groups, 8, 128), BF), vm((groups, 8, 128), BF), vm((2, img, kvd // 2), BF),
            vm((tps, rows, 128), BF), vm((tps, rows, 128), BF), vm((8, 128), F32), vm((pps - 1, 8, 128), F32)]
-        + [dma(7 + parts), dma(7), dma(7), dma(7), dma(7), dma(7), dma(7), dma(3), dma(3),
+        + [dma(7 + parts), dma(8), dma(8), dma(8), dma(8), dma(8), dma(8), dma(3), dma(3),
            dma(tps - 1), dma(tps - 1), dma(2), dma(pps - 1), dma(pps - 1)]
     )
+    in_hbm = lambda a: pltpu.with_memory_space_constraint(a, pltpu.HBM)
     values, grads = pl.pallas_call(
-        functools.partial(kernel, (groups, tps, pps, parts)),
+        functools.partial(kernel, (groups, tps, pps, parts, cut)),
         out_shape=(
             jax.ShapeDtypeStruct((rows, kvd), BF),
             jax.ShapeDtypeStruct((grows, dvis), BF),
@@ -373,7 +400,10 @@
             collective_id=0, has_side_effects=True, vmem_limit_bytes=48 * 1024 * 1024
         ),
     )(
-        target.reshape(1, img), slot_place.reshape(1, slots), loss_mask, vision, w_proj, w_value, text_embed, cotangent
+        *map(
+            in_hbm,
+            (target.reshape(1, img), slot_place.reshape(1, slots), loss_mask, vision, w_proj, w_value, text_embed, cotangent),
+        )
     )
     return values[None], grads[None]
 

time: 55.1 us -> 47.7 us (0.87)
  local copies, waits for them, and re-layouts: 7.91 us -> 1.25 us
    unnamed x16 -> x2, local copies, waits for them, and re-layouts: 7.91 us -> 1.25 us
where the time goes in v2:
time: 47.7 us; the launch traced here: 47.5 us
  Pallas kernels  45.6 us (96%)
  local copies, waits for them, and re-layouts  1.25 us (3%)
  between operations  0.64 us (1%)
    pallas_call x1, Pallas kernels, body(): pl.pallas_call(functools.partial(kernel, (groups, tps, pps, parts, cut)),...  45.6 us
    unnamed x2, local copies, waits for them, and re-layouts  1.25 us

profile of v2, /device:TPU:1, one launch (start us, length us, event | category | flops | bytes accessed | tf_op | source)
XLA Modules:
  0.0 47.5 jit_solution(14566757968601553339)
XLA Ops:
  0.6 45.6 %shard_map.95 = (bf16[32,1024]{1,0:T(8,128)(2,1)S(1)}, bf16[8,3200]{1,0:T(8,128)(2,1)S(1)}) custom-call(s32[1,64]{1,0:T(1,128)} %bitcast.6, s32[1,128]{1,0:T(1,128)} %bitcast.7, s32[1,256]{1,0:T(1,128)} %loss.1, bf16[1,64,3200]{2,1,0:T(8,128)(2,1)} %vision.1, bf16[3200,1024]{1,0:T(8,128)(2,1)} %w_proj.1, bf16[1024,1024]{1,0:T(8,128)(2,1)} %w_value.1, ...), custom_call_target="tpu_custom_call" | custom-call | tf_op jit(solution)/shard_map/pallas_call | solution.py:390
  46.3 0.6 %copy.12 = bf16[1,32,1024]{2,1,0:T(8,128)(2,1)} copy(bf16[1,32,1024]{2,1,0:T(8,128)(2,1)S(1)} %bitcast.4) | data formatting | bytes 131072
  46.9 0.6 %copy.13 = bf16[1,8,3200]{2,1,0:T(8,128)(2,1)} copy(bf16[1,8,3200]{2,1,0:T(8,128)(2,1)S(1)} %bitcast.5) | data formatting | bytes 102400

commit v3 on v2

--- a/solution.py
+++ b/solution.py
@@ -30,6 +30,10 @@
 def to_col(row):
     n = row.shape[1]
     return jnp.sum(jnp.where(iota((n, n), 0) == iota((n, n), 1), row, 0), axis=1, keepdims=True)
+
+
+def collected(ref, sem, n):
+    pltpu.make_async_copy(ref.at[pl.ds(0, n)], ref.at[pl.ds(0, n)], sem).wait()
 
 
 class Reduce:
@@ -51,11 +55,12 @@
         ]
         self.copies = [
             pltpu.make_async_remote_copy(
-                src, dst, send.at[i], recv.at[i], device_id={"tp": env[way]}, device_id_type=MESH
+                src, dst, send.at[1 if i > 5 else 0], recv.at[i if i < 2 else 2 if i < 6 else i - 3],
+                device_id={"tp": env[way]}, device_id_type=MESH,
             )
             for i, (src, dst, way) in enumerate(table)
         ]
-        self.r1, self.fdn, self.fup = r1, fdn, fup
+        self.r1, self.fdn, self.fup, self.send, self.recv = r1, fdn, fup, send, recv
 
     def start_pair(self, s):
         half = self.half
@@ -86,8 +91,7 @@
 
     def end(self):
         env = self.env
-        for i in (2, 3, 4, 5):
-            self.copies[i].wait_recv()
+        collected(self.pr, self.recv.at[2], 2)
         return (
             self.mine[env["hi"]]
             + self.pr[env["hi"]].astype(F32)
@@ -96,8 +100,8 @@
         )
 
     def drain(self):
-        for c in self.copies:
-            c.wait_send()
+        collected(self.pb, self.send.at[1], self.pb.shape[0])
+        collected(self.sb, self.send.at[0], 3)
 
 
 def kernel(
@@ -137,12 +141,14 @@
     ] + [(w_proj.at[pl.ds(i * kchunk, kchunk)], wp_v.at[pl.ds(i * kchunk, kchunk)]) for i in range(parts)]
     pairs += [(w_value, wv_v), (text.at[0], text_v)]
     loads = [pltpu.make_async_copy(s, d, load_sem.at[i]) for i, (s, d) in enumerate(pairs)]
-    for c in loads:
+    for c in loads[:4]:
         c.start()
     l_cot, l_vision, l_proj, l_value, l_text = loads[3], loads[4], loads[5:-2], loads[-2], loads[-1]
     barrier = pltpu.get_barrier_semaphore()
     for p in peers:
         pl.semaphore_signal(barrier, inc=1, device_id={"grp": p}, device_id_type=MESH)
+    for c in loads[4:]:
+        c.start()
     for i in range(1, tps):
         pl.semaphore_signal(barrier, inc=1, device_id={"tp": lax.rem(tp + i, tps)}, device_id_type=MESH)
     for i in range(1, pps):
@@ -168,8 +174,9 @@
     meta = jnp.where(r8 == 0, counts, jnp.where(r8 == 1, mask_row, jnp.where(r8 == 2, mask_sum, 0.0)))
     xmeta[...] = meta
 
-    d_i, d_l = iota((4 * slots, 4 * slots), 0), iota((4 * slots, 4 * slots), 1)
-    shuffle = flag(d_l == slots * ((d_i // 4) % 4) + 4 * (d_i // 16) + d_i % 4).astype(BF)
+    d_i = iota((4 * slots, 1), 0)
+    d_from = slots * ((d_i // 4) % 4) + 4 * (d_i // 16) + d_i % 4
+    shuffle = flag(iota((4 * slots, 4 * slots), 1) == d_from).astype(BF)
     l_cot.wait()
     y = mm(at_slot.astype(BF), cot_v[...]).astype(BF)
     ystack = jnp.concatenate([y[:, 128 * j : 128 * (j + 1)] for j in range(4)], axis=0)
@@ -211,9 +218,6 @@
                 device_id={"grp": p}, device_id_type=MESH,
             ).start()
 
-    def collected(ref, sem, n):
-        pltpu.make_async_copy(ref.at[pl.ds(0, n)], ref.at[pl.ds(0, n)], sem).wait()
-
     spread(xcot, rcot, 0, False)
 
     l_text.wait()
@@ -258,26 +262,33 @@
     half_cols = lambda c: pl.ds(pl.multiple_of(c * half_kv, 128), half_kv)
     for n in range(0, width, 256):
         emb_acc[:, n : n + 256] = mm_nt(mine, wv_v[n : n + 256, half_cols(core)])
+    swap.wait_recv()
     red_t.relay(0)
     red_t.relay(1)
-    swap.wait_recv()
     other = chalf[1 - core]
     for n in range(0, width, 256):
         emb_acc[:, n : n + 256] += mm_nt(other, wv_v[n : n + 256, half_cols(1 - core)])
     d_img = emb_acc[...].astype(BF)
 
+    def grad_part(lo, up):
+        res = mm_nt(d_img, wp_v[lo:up, :])
+        for t in range(tps):
+            gpf[t % 2, t // 2, :, lo:up] = res[8 * t : 8 * t + 8]
+
+    grad_part(0, cut // 2)
+    grad_part(cut // 2, cut)
+    red_g.start_pair(0)
+
     vals = red_i.end().reshape(img, 128).astype(BF)
     r_slot = flag(iota((8 * groups, img), 0) == 8 * t_row + k_row).astype(BF)
     ximg[...] = mm(r_slot, vals).reshape(groups, 8, 128).astype(BF)
     spread(ximg, rimg, 2, False)
 
-    for s, bounds in enumerate(((0, cut // 2, cut), (cut, cut + (dvis - cut) // 256 * 128, dvis))):
-        for lo, up in zip(bounds[:-1], bounds[1:]):
-            res = mm_nt(d_img, wp_v[lo:up, :])
-            for t in range(tps):
-                gpf[t % 2, t // 2, :, lo:up] = res[8 * t : 8 * t + 8]
-        red_g.start_pair(s)
+    mid = cut + (dvis - cut) // 256 * 128
+    grad_part(cut, mid)
     red_g.first(0)
+    grad_part(mid, dvis)
+    red_g.start_pair(1)
 
     collected(rmeta, a_recv.at[1], groups - 1)
     rmeta[pl.ds(grp, 1)] = xmeta[...][None]
@@ -298,7 +309,7 @@
     for i in range(1, pps):
         tot_copies.append(
             pltpu.make_async_remote_copy(
-                tot_s, tot_r.at[i - 1], p_send.at[i - 1], p_recv.at[i - 1],
+                tot_s, tot_r.at[i - 1], p_send.at[0], p_recv.at[0],
                 device_id={"pp": lax.rem(pp + i, pps)}, device_id_type=MESH,
             )
         )
@@ -324,7 +335,7 @@
         peer = lax.rem(tp + i, tps)
         z_copies.append(
             pltpu.make_async_remote_copy(
-                zs.at[peer], zr.at[tp], z_send.at[i - 1], z_recv.at[i - 1], device_id={"tp": peer}, device_id_type=MESH
+                zs.at[peer], zr.at[tp], z_send.at[0], z_recv.at[0], device_id={"tp": peer}, device_id_type=MESH
             )
         )
         z_copies[-1].start()
@@ -333,15 +344,13 @@
     red_g.relay(1)
     text_vals = red_t.end().reshape(rows_out, kvd)
     is_img = jnp.sum(flag(iota((rows_out, 8 * groups), 0) + rows_out * tp == pos8), axis=1, keepdims=True)
-    for c in z_copies:
-        c.wait_recv()
+    collected(zr, z_recv.at[0], tps - 1)
     zr[pl.ds(tp, 1)] = zs[pl.ds(tp, 1)]
     for t in range(tps):
         cols = slice(128 * t, 128 * t + 128)
         values_out[:, cols] = jnp.where(is_img > 0.5, zr[t].astype(F32), text_vals[:, cols]).astype(BF)
 
-    for c in tot_copies:
-        c.wait_recv()
+    collected(tot_r, p_recv.at[0], pps - 1)
     text_total = tot_s[...]
     for i in range(1, pps):
         text_total = text_total + tot_r[i - 1]
@@ -354,8 +363,8 @@
     collected(rmeta, a_send.at[1], groups - 1)
     collected(ximg, a_send.at[2], groups - 1)
     swap.wait_send()
-    for c in z_copies + tot_copies:
-        c.wait_send()
+    collected(zs, z_send.at[0], tps - 1)
+    collected(tot_r, p_send.at[0], pps - 1)
 
 
 def body(vision, text_embed, target, slot_place, loss_mask, w_proj, w_value, cotangent):
@@ -383,8 +392,8 @@
         + [vm((groups, 16, 128), BF), vm((groups, 16, 128), BF), vm((8, 128), F32), vm((groups, 8, 128), F32),
            vm((groups, 8, 128), BF), vm((groups, 8, 128), BF), vm((2, img, kvd // 2), BF),
            vm((tps, rows, 128), BF), vm((tps, rows, 128), BF), vm((8, 128), F32), vm((pps - 1, 8, 128), F32)]
-        + [dma(7 + parts), dma(8), dma(8), dma(8), dma(8), dma(8), dma(8), dma(3), dma(3),
-           dma(tps - 1), dma(tps - 1), dma(2), dma(pps - 1), dma(pps - 1)]
+        + [dma(7 + parts), dma(2), dma(5), dma(2), dma(5), dma(2), dma(5), dma(3), dma(3),
+           dma(1), dma(1), dma(2), dma(1), dma(1)]
     )
     in_hbm = lambda a: pltpu.with_memory_space_constraint(a, pltpu.HBM)
     values, grads = pl.pallas_call(

time: 47.7 us -> 46.3 us (0.971)
  Pallas kernels: 45.6 us -> 44.3 us
    pallas_call x1, Pallas kernels: 45.6 us -> 44.3 us  [body(): pl.pallas_call(functools.partial(kernel, (groups, tps, pps, parts, cut)),...]
where the time goes in v3:
time: 46.3 us; the launch traced here: 46.2 us
  Pallas kernels  44.3 us (96%)
  local copies, waits for them, and re-layouts  1.25 us (3%)
  between operations  0.64 us (1%)
    pallas_call x1, Pallas kernels, body(): pl.pallas_call(functools.partial(kernel, (groups, tps, pps, parts, cut)),...  44.3 us
    unnamed x2, local copies, waits for them, and re-layouts  1.25 us

profile of v3, /device:TPU:1, one launch (start us, length us, event | category | flops | bytes accessed | tf_op | source)
XLA Modules:
  0.0 46.2 jit_solution(4093515429954040435)
XLA Ops:
  0.6 44.3 %shard_map.95 = (bf16[32,1024]{1,0:T(8,128)(2,1)S(1)}, bf16[8,3200]{1,0:T(8,128)(2,1)S(1)}) custom-call(s32[1,64]{1,0:T(1,128)} %bitcast.6, s32[1,128]{1,0:T(1,128)} %bitcast.7, s32[1,256]{1,0:T(1,128)} %loss.1, bf16[1,64,3200]{2,1,0:T(8,128)(2,1)} %vision.1, bf16[3200,1024]{1,0:T(8,128)(2,1)} %w_proj.1, bf16[1024,1024]{1,0:T(8,128)(2,1)} %w_value.1, ...), custom_call_target="tpu_custom_call" | custom-call | tf_op jit(solution)/shard_map/pallas_call | solution.py:399
  44.9 0.6 %copy.12 = bf16[1,32,1024]{2,1,0:T(8,128)(2,1)} copy(bf16[1,32,1024]{2,1,0:T(8,128)(2,1)S(1)} %bitcast.4) | data formatting | bytes 131072
  45.6 0.6 %copy.13 = bf16[1,8,3200]{2,1,0:T(8,128)(2,1)} copy(bf16[1,8,3200]{2,1,0:T(8,128)(2,1)S(1)} %bitcast.5) | data formatting | bytes 102400

commit v4 on v3

--- a/solution.py
+++ b/solution.py
@@ -141,13 +141,13 @@
     ] + [(w_proj.at[pl.ds(i * kchunk, kchunk)], wp_v.at[pl.ds(i * kchunk, kchunk)]) for i in range(parts)]
     pairs += [(w_value, wv_v), (text.at[0], text_v)]
     loads = [pltpu.make_async_copy(s, d, load_sem.at[i]) for i, (s, d) in enumerate(pairs)]
-    for c in loads[:4]:
+    for c in loads[:-2]:
         c.start()
     l_cot, l_vision, l_proj, l_value, l_text = loads[3], loads[4], loads[5:-2], loads[-2], loads[-1]
     barrier = pltpu.get_barrier_semaphore()
     for p in peers:
         pl.semaphore_signal(barrier, inc=1, device_id={"grp": p}, device_id_type=MESH)
-    for c in loads[4:]:
+    for c in loads[-2:]:
         c.start()
     for i in range(1, tps):
         pl.semaphore_signal(barrier, inc=1, device_id={"tp": lax.rem(tp + i, tps)}, device_id_type=MESH)
@@ -223,7 +223,8 @@
     l_text.wait()
     rows_out = seq // tps
     hr = rows_out // 2
-    for n in range(4):
+
+    def text_part(n):
         cols = pl.ds(n * 256, 256)
         res = mm(text_v[...], wv_v[:, cols])
         for t in range(tps):
@@ -231,10 +232,15 @@
                 r0 = t * rows_out + s * hr
                 tpf[t % 2, t // 2, s, :, cols] = res[r0 : r0 + hr]
 
+    text_part(0)
+    text_part(1)
+
     red_i.first(0)
     red_i.first(1)
     red_i.direct(0)
     red_i.direct(1)
+    for n in range(2, kvd // 256):
+        text_part(n)
     red_t.start_pair(0)
     red_t.start_pair(1)
     spread(xmeta, rmeta, 1, True)
@@ -275,14 +281,15 @@
         for t in range(tps):
             gpf[t % 2, t // 2, :, lo:up] = res[8 * t : 8 * t + 8]
 
-    grad_part(0, cut // 2)
-    grad_part(cut // 2, cut)
-    red_g.start_pair(0)
+    first = cut // 256 * 128
+    grad_part(0, first)
 
     vals = red_i.end().reshape(img, 128).astype(BF)
     r_slot = flag(iota((8 * groups, img), 0) == 8 * t_row + k_row).astype(BF)
     ximg[...] = mm(r_slot, vals).reshape(groups, 8, 128).astype(BF)
     spread(ximg, rimg, 2, False)
+    grad_part(first, cut)
+    red_g.start_pair(0)
 
     mid = cut + (dvis - cut) // 256 * 128
     grad_part(cut, mid)
@@ -367,12 +374,23 @@
     collected(tot_r, p_send.at[0], pps - 1)
 
 
+def put_out(values, grads, values_out, grads_out, sems):
+    copies = [
+        pltpu.make_async_copy(values, values_out.at[0], sems.at[0]),
+        pltpu.make_async_copy(grads, grads_out.at[0], sems.at[1]),
+    ]
+    for c in copies:
+        c.start()
+    for c in copies:
+        c.wait()
+
+
 def body(vision, text_embed, target, slot_place, loss_mask, w_proj, w_value, cotangent):
     groups, tps, pps = lax.axis_size("grp"), lax.axis_size("tp"), lax.axis_size("pp")
     img, dvis, width = vision.shape[1], vision.shape[2], w_proj.shape[1]
     seq, kvd, slots = text_embed.shape[1], w_value.shape[1], slot_place.shape[2]
     chips, parts = tps // 2, 5
-    cut = dvis // 256 * 128
+    cut = dvis * 3 // 5 // 128 * 128
     rows, grows = seq // tps, img // tps
     vm = pltpu.VMEM
     dma = lambda *s: pltpu.SemaphoreType.DMA(s)
@@ -414,7 +432,14 @@
             (target.reshape(1, img), slot_place.reshape(1, slots), loss_mask, vision, w_proj, w_value, text_embed, cotangent),
         )
     )
-    return values[None], grads[None]
+    return pl.pallas_call(
+        put_out,
+        out_shape=(jax.ShapeDtypeStruct((1, rows, kvd), BF), jax.ShapeDtypeStruct((1, grows, dvis), BF)),
+        in_specs=[pl.BlockSpec(memory_space=pltpu.VMEM)] * 2,
+        out_specs=(pl.BlockSpec(memory_space=pltpu.HBM), pl.BlockSpec(memory_space=pltpu.HBM)),
+        scratch_shapes=[dma(2)],
+        compiler_params=pltpu.CompilerParams(vmem_limit_bytes=4 * 1024 * 1024),
+    )(values, grads)
 
 
 def solution(mesh):

time: 46.3 us -> 45.5 us (0.983)
  local copies, waits for them, and re-layouts: 1.25 us -> 0 us
  Pallas kernels: 44.3 us -> 44.8 us
    unnamed x2 -> x0, local copies, waits for them, and re-layouts: 1.25 us -> none
    pallas_call x0 -> x1, Pallas kernels: none -> 0.66 us  [body(): pl.pallas_call(put_out, out_shape=(jax.ShapeDtypeStruct((1, rows, kvd), B...]
where the time goes in v4:
time: 45.5 us; the launch traced here: 45.4 us
  Pallas kernels  44.8 us (98%)
  between operations  0.64 us (1%)
    pallas_call x1, Pallas kernels, body(): pl.pallas_call(functools.partial(kernel, (groups, tps, pps, parts, cut)),...  44.1 us

profile of v4, /device:TPU:1, one launch (start us, length us, event | category | flops | bytes accessed | tf_op | source)
XLA Modules:
  0.0 45.4 jit_solution(15902682724578954751)
XLA Ops:
  0.6 44.1 %shard_map.95 = (bf16[32,1024]{1,0:T(8,128)(2,1)S(1)}, bf16[8,3200]{1,0:T(8,128)(2,1)S(1)}) custom-call(s32[1,64]{1,0:T(1,128)} %bitcast.2, s32[1,128]{1,0:T(1,128)} %bitcast.3, s32[1,256]{1,0:T(1,128)} %loss.1, bf16[1,64,3200]{2,1,0:T(8,128)(2,1)} %vision.1, bf16[3200,1024]{1,0:T(8,128)(2,1)} %w_proj.1, bf16[1024,1024]{1,0:T(8,128)(2,1)} %w_value.1, ...), custom_call_target="tpu_custom_call" | custom-call | tf_op jit(solution)/shard_map/pallas_call | solution.py:417
  44.8 0.7 %shard_map.96 = (bf16[1,32,1024]{2,1,0:T(8,128)(2,1)}, bf16[1,8,3200]{2,1,0:T(8,128)(2,1)}) custom-call(bf16[32,1024]{1,0:T(8,128)(2,1)S(1)} %get-tuple-element.4.values, bf16[8,3200]{1,0:T(8,128)(2,1)S(1)} %get-tuple-element.5.grads), custom_call_target="tpu_custom_call" | custom-call | tf_op jit(solution)/shard_map/pallas_call | solution.py:435

commit v5 on v4

--- a/solution.py
+++ b/solution.py
@@ -37,35 +37,37 @@
 
 
 class Reduce:
-    def __init__(self, env, half, pf, pb, pr, sb, r1, fdn, fup, send, recv):
-        self.env, self.half = env, half
+    def __init__(self, env, half, pieces, pf, pb, pr, sb, r1, fdn, fup, send, recv):
+        self.env, self.half, self.pieces = env, half, pieces
         self.pf, self.pb, self.pr, self.sb = pf, pb, pr, sb
         self.mine = pf.at[env["core"]]
         h_up, h_dn, h_op = env["h_up"], env["h_dn"], env["h_op"]
         own = lambda h, s: half(sb.at[h], s)
-        table = [
-            (own(h_op, 0), half(r1, 0), "up"),
-            (own(h_op, 1), half(r1, 1), "dn"),
-            (own(h_dn, 0), half(fup, 0), "dn"),
-            (own(h_up, 1), half(fdn, 1), "up"),
-            (own(h_up, 0), half(fdn, 0), "up"),
-            (own(h_dn, 1), half(fup, 1), "dn"),
-            (half(pb, 0), half(pr, 0), "partner"),
-            (half(pb, 1), half(pr, 1), "partner"),
+        n = len(pieces[0])
+
+        def copy(src, dst, way, out, got):
+            return pltpu.make_async_remote_copy(
+                src, dst, send.at[out], recv.at[got], device_id={"tp": env[way]}, device_id_type=MESH
+            )
+
+        ways = (("up", h_up, fdn), ("dn", h_dn, fup))
+        self.pair = [copy(half(pb, s), half(pr, s), "partner", 1, s) for s in range(2)]
+        self.firsts = [
+            [copy(p(sb.at[h_op]), p(r1), ways[s][0], 0, 3 + s * n + u) for u, p in enumerate(pieces[s])]
+            for s in range(2)
         ]
-        self.copies = [
-            pltpu.make_async_remote_copy(
-                src, dst, send.at[1 if i > 5 else 0], recv.at[i if i < 2 else 2 if i < 6 else i - 3],
-                device_id={"tp": env[way]}, device_id_type=MESH,
-            )
-            for i, (src, dst, way) in enumerate(table)
+        self.directs = [
+            copy(own(ways[1 - s][1], s), half(ways[1 - s][2], s), ways[1 - s][0], 0, 2) for s in range(2)
+        ]
+        self.relays = [
+            [copy(p(sb.at[ways[s][1]]), p(ways[s][2]), ways[s][0], 0, 2) for p in pieces[s]] for s in range(2)
         ]
         self.r1, self.fdn, self.fup, self.send, self.recv = r1, fdn, fup, send, recv
 
     def start_pair(self, s):
         half = self.half
         half(self.pb, s)[...] = half(self.pf.at[1 - self.env["core"]], s)[...].astype(BF)
-        self.copies[6 + s].start()
+        self.pair[s].start()
 
     def pair_sum(self, h, s):
         half = self.half
@@ -73,21 +75,23 @@
 
     def first(self, s):
         h = self.env["h_op"]
-        self.copies[6 + s].wait_recv()
+        self.pair[s].wait_recv()
         self.half(self.sb.at[h], s)[...] = self.pair_sum(h, s).astype(BF)
-        self.copies[s].start()
+        for c in self.firsts[s]:
+            c.start()
 
     def direct(self, s):
         h = self.env["h_dn" if s == 0 else "h_up"]
         self.half(self.sb.at[h], s)[...] = self.pair_sum(h, s).astype(BF)
-        self.copies[2 + s].start()
+        self.directs[s].start()
 
     def relay(self, s):
         h = self.env["h_up" if s == 0 else "h_dn"]
-        v = self.pair_sum(h, s)
-        self.copies[s].wait_recv()
-        self.half(self.sb.at[h], s)[...] = (v + self.half(self.r1, s)[...].astype(F32)).astype(BF)
-        self.copies[4 + s].start()
+        for p, got, out in zip(self.pieces[s], self.firsts[s], self.relays[s]):
+            v = p(self.mine.at[h])[...] + p(self.pr.at[h])[...].astype(F32)
+            got.wait_recv()
+            p(self.sb.at[h])[...] = (v + p(self.r1)[...].astype(F32)).astype(BF)
+            out.start()
 
     def end(self):
         env = self.env
@@ -172,7 +176,7 @@
     mask_sum = jnp.sum(loss_f, axis=1, keepdims=True)
     r8 = iota((8, 128), 0)
     meta = jnp.where(r8 == 0, counts, jnp.where(r8 == 1, mask_row, jnp.where(r8 == 2, mask_sum, 0.0)))
-    xmeta[...] = meta
+    xmeta[...] = meta.astype(BF)
 
     d_i = iota((4 * slots, 1), 0)
     d_from = slots * ((d_i // 4) % 4) + 4 * (d_i // 16) + d_i % 4
@@ -202,9 +206,12 @@
     lead = lambda ref, s: ref.at[..., s, :, :] if len(ref.shape) == 4 else ref.at[s]
     span = (pl.ds(0, cut), pl.ds(cut, dvis - cut))
     lane_cut = lambda ref, s: ref.at[..., span[s]]
-    red_i = Reduce(env, lead, ipf, ipb, ipr, isb, ir1, ifd, ifu, i_send, i_recv)
-    red_t = Reduce(env, lead, tpf, tpb, tpr, tsb, tr1, tfd, tfu, t_send, t_recv)
-    red_g = Reduce(env, lane_cut, gpf, gpb, gpr, gsb, gr1, gfd, gfu, g_send, g_recv)
+    whole = [[lambda ref, s=s: lead(ref, s)] for s in range(2)]
+    mids = ((0, cut // 256 * 128, cut), (cut, cut + (dvis - cut) // 256 * 128, dvis))
+    parts_g = [[lambda ref, lo=lo, up=up: ref.at[..., pl.ds(lo, up - lo)] for lo, up in zip(m[:-1], m[1:])] for m in mids]
+    red_i = Reduce(env, lead, whole, ipf, ipb, ipr, isb, ir1, ifd, ifu, i_send, i_recv)
+    red_t = Reduce(env, lead, whole, tpf, tpb, tpr, tsb, tr1, tfd, tfu, t_send, t_recv)
+    red_g = Reduce(env, lane_cut, parts_g, gpf, gpb, gpr, gsb, gr1, gfd, gfu, g_send, g_recv)
 
     pl.semaphore_wait(barrier, (tps - 1) + (groups - 1) + (pps - 1))
 
@@ -243,7 +250,6 @@
         text_part(n)
     red_t.start_pair(0)
     red_t.start_pair(1)
-    spread(xmeta, rmeta, 1, True)
     red_t.first(0)
     red_t.first(1)
     red_i.relay(0)
@@ -264,6 +270,8 @@
         chalf.at[core], chalf.at[core], s_sem.at[0], s_sem.at[1], device_id={"tp": env["partner"]}, device_id_type=MESH
     )
     swap.start()
+
+    spread(xmeta, rmeta, 1, True)
 
     half_cols = lambda c: pl.ds(pl.multiple_of(c * half_kv, 128), half_kv)
     for n in range(0, width, 256):
@@ -284,8 +292,8 @@
     first = cut // 256 * 128
     grad_part(0, first)
 
+    r_slot = flag(iota((8 * groups, img), 0) == 8 * t_row + k_row).astype(BF)
     vals = red_i.end().reshape(img, 128).astype(BF)
-    r_slot = flag(iota((8 * groups, img), 0) == 8 * t_row + k_row).astype(BF)
     ximg[...] = mm(r_slot, vals).reshape(groups, 8, 128).astype(BF)
     spread(ximg, rimg, 2, False)
     grad_part(first, cut)
@@ -297,9 +305,12 @@
     grad_part(mid, dvis)
     red_g.start_pair(1)
 
+    red_g.first(1)
+    red_g.direct(1)
+
     collected(rmeta, a_recv.at[1], groups - 1)
     rmeta[pl.ds(grp, 1)] = xmeta[...][None]
-    metas = rmeta[...].reshape(8 * groups, 128).astype(BF)
+    metas = rmeta[...].astype(F32).reshape(8 * groups, 128).astype(BF)
     e_i, e_l = iota((groups, 8 * groups), 0), iota((groups, 8 * groups), 1)
     c_mat = mm(flag(e_l == 8 * e_i).astype(BF), metas)
     m_mat = mm(flag(e_l == 8 * e_i + 1).astype(BF), metas)
@@ -320,11 +331,8 @@
                 device_id={"pp": lax.rem(pp + i, pps)}, device_id_type=MESH,
             )
         )
-    red_g.first(1)
     for c in tot_copies:
         c.start()
-    red_g.direct(0)
-    red_g.direct(1)
 
     x_l, x_i = iota((slots, 8 * groups), 1), iota((slots, 8 * groups), 0)
     holds = (x_i == cap * (x_l // 8) + x_l % 8) & (x_l % 8 < cap)
@@ -347,6 +355,7 @@
         )
         z_copies[-1].start()
 
+    red_g.direct(0)
     red_g.relay(0)
     red_g.relay(1)
     text_vals = red_t.end().reshape(rows_out, kvd)
@@ -407,10 +416,10 @@
         + reduce_bufs((2, rows // 2, kvd))
         + reduce_bufs((2, img // 2, 128))
         + reduce_bufs((grows, dvis))
-        + [vm((groups, 16, 128), BF), vm((groups, 16, 128), BF), vm((8, 128), F32), vm((groups, 8, 128), F32),
+        + [vm((groups, 16, 128), BF), vm((groups, 16, 128), BF), vm((8, 128), BF), vm((groups, 8, 128), BF),
            vm((groups, 8, 128), BF), vm((groups, 8, 128), BF), vm((2, img, kvd // 2), BF),
            vm((tps, rows, 128), BF), vm((tps, rows, 128), BF), vm((8, 128), F32), vm((pps - 1, 8, 128), F32)]
-        + [dma(7 + parts), dma(2), dma(5), dma(2), dma(5), dma(2), dma(5), dma(3), dma(3),
+        + [dma(7 + parts), dma(2), dma(5), dma(2), dma(5), dma(2), dma(7), dma(3), dma(3),
            dma(1), dma(1), dma(2), dma(1), dma(1)]
     )
     in_hbm = lambda a: pltpu.with_memory_space_constraint(a, pltpu.HBM)

time: 45.5 us -> 45.5 us (level)
  no operation moved by 1% of the time
where the time goes in v5:
time: 45.5 us; the launch traced here: 45.4 us
  Pallas kernels  44.7 us (98%)
  between operations  0.64 us (1%)
    pallas_call x1, Pallas kernels, body(): pl.pallas_call(functools.partial(kernel, (groups, tps, pps, parts, cut)),...  44.1 us

profile of v5, /device:TPU:1, one launch (start us, length us, event | category | flops | bytes accessed | tf_op | source)
XLA Modules:
  0.0 45.4 jit_solution(2150588582514821190)
XLA Ops:
  0.6 44.1 %shard_map.95 = (bf16[32,1024]{1,0:T(8,128)(2,1)S(1)}, bf16[8,3200]{1,0:T(8,128)(2,1)S(1)}) custom-call(s32[1,64]{1,0:T(1,128)} %bitcast.2, s32[1,128]{1,0:T(1,128)} %bitcast.3, s32[1,256]{1,0:T(1,128)} %loss.1, bf16[1,64,3200]{2,1,0:T(8,128)(2,1)} %vision.1, bf16[3200,1024]{1,0:T(8,128)(2,1)} %w_proj.1, bf16[1024,1024]{1,0:T(8,128)(2,1)} %w_value.1, ...), custom_call_target="tpu_custom_call" | custom-call | tf_op jit(solution)/shard_map/pallas_call | solution.py:426
  44.7 0.7 %shard_map.96 = (bf16[1,32,1024]{2,1,0:T(8,128)(2,1)}, bf16[1,8,3200]{2,1,0:T(8,128)(2,1)}) custom-call(bf16[32,1024]{1,0:T(8,128)(2,1)S(1)} %get-tuple-element.4.values, bf16[8,3200]{1,0:T(8,128)(2,1)S(1)} %get-tuple-element.5.grads), custom_call_target="tpu_custom_call" | custom-call | tf_op jit(solution)/shard_map/pallas_call | solution.py:444

commit v6 on v5

--- a/solution.py
+++ b/solution.py
@@ -301,9 +301,9 @@
 
     mid = cut + (dvis - cut) // 256 * 128
     grad_part(cut, mid)
-    red_g.first(0)
     grad_part(mid, dvis)
     red_g.start_pair(1)
+    red_g.first(0)
 
     red_g.first(1)
     red_g.direct(1)

time: 45.5 us -> 45.4 us (level)
  no operation moved by 1% of the time
where the time goes in v6:
time: 45.4 us; the launch traced here: 45.3 us
  Pallas kernels  44.6 us (98%)
  between operations  0.64 us (1%)
    pallas_call x1, Pallas kernels, body(): pl.pallas_call(functools.partial(kernel, (groups, tps, pps, parts, cut)),...  44 us

profile of v6, /device:TPU:1, one launch (start us, length us, event | category | flops | bytes accessed | tf_op | source)
XLA Modules:
  0.0 45.3 jit_solution(17349900121834353929)
XLA Ops:
  0.6 44.0 %shard_map.95 = (bf16[32,1024]{1,0:T(8,128)(2,1)S(1)}, bf16[8,3200]{1,0:T(8,128)(2,1)S(1)}) custom-call(s32[1,64]{1,0:T(1,128)} %bitcast.2, s32[1,128]{1,0:T(1,128)} %bitcast.3, s32[1,256]{1,0:T(1,128)} %loss.1, bf16[1,64,3200]{2,1,0:T(8,128)(2,1)} %vision.1, bf16[3200,1024]{1,0:T(8,128)(2,1)} %w_proj.1, bf16[1024,1024]{1,0:T(8,128)(2,1)} %w_value.1, ...), custom_call_target="tpu_custom_call" | custom-call | tf_op jit(solution)/shard_map/pallas_call | solution.py:426
  44.6 0.7 %shard_map.96 = (bf16[1,32,1024]{2,1,0:T(8,128)(2,1)}, bf16[1,8,3200]{2,1,0:T(8,128)(2,1)}) custom-call(bf16[32,1024]{1,0:T(8,128)(2,1)S(1)} %get-tuple-element.4.values, bf16[8,3200]{1,0:T(8,128)(2,1)S(1)} %get-tuple-element.5.grads), custom_call_target="tpu_custom_call" | custom-call | tf_op jit(solution)/shard_map/pallas_call | solution.py:444
